TPU v7x, 32 devices: a whole 2x2x4 slice. The times are simulated.
32 devices in a mesh: section: 4 (over y, core), fsdp: 8 (over z, x).
Axes of the slice: x: 2, y: 2, z: 4, core: 2. Of those that a mesh axis runs over, the one named last changes fastest.
Arguments:
- hidden_in: bfloat16 [1024, 4096], P('fsdp'), may hold values from -6 to 6
- out_grad: bfloat16 [1024, 4096], P('fsdp'), may hold values from -6 to 6
- fast_in: float32 [4, 4096, 1024], P('section', 'fsdp'), may hold values from -6 to 6
- fast_out: float32 [4, 1024, 4096], P('section', None, 'fsdp'), may hold values from -6 to 6
- slow_in: float32 [4, 4096, 1024], P('section', 'fsdp'), may hold values from -6 to 6
- slow_out: float32 [4, 1024, 4096], P('section', None, 'fsdp'), may hold values from -6 to 6
Outputs:
- section_out: bfloat16 [4, 1024, 4096], P('section', 'fsdp')
- input_grad: bfloat16 [4, 1024, 4096], P('section', 'fsdp')
- synced_in: float32 [4, 4096, 1024], P('section', 'fsdp')
- synced_out: float32 [4, 1024, 4096], P('section', None, 'fsdp')
All inputs are finite; a program needn't handle non-finite values.
Results may differ from a plain program's by a relative error of at most 0.014.
Values may be sent and summed in bfloat16 or wider, within the bound.
No kernel may reach another device: no remote copies, remote signals or barrier semaphores. Data moves between devices by JAX's collectives and lax.ppermute only.
A program may use at most 896 MiB of HBM per device.

v0:
```python
import math
import jax
import jax.numpy as jnp
from jax import lax
from jax.sharding import PartitionSpec as P

epsilon = 1e-05
fast_rate = 0.5
preview_mix = 0.5


def from_behind(value, axis, steps):
    count = lax.axis_size(axis)
    leading, last = (max(0, -steps), min(count, count - steps))
    return lax.ppermute(value, axis, [(source, source + steps) for source in range(leading, last)])


def contract_last(left_rows, right_rows):
    return lax.dot_general(
        left_rows, right_rows, (((1,), (1,)), ((), ())), preferred_element_type=jnp.float32
    )


def contract_first(left_rows, right_rows):
    return lax.dot_general(
        left_rows, right_rows, (((0,), (0,)), ((), ())), preferred_element_type=jnp.float32
    )


def prepare(hidden, weight_in):
    widened = hidden.astype(jnp.float32)
    inverse_rms = lax.rsqrt(jnp.mean(widened * widened, axis=-1, keepdims=True) + epsilon)
    normed = (widened * inverse_rms).astype(jnp.bfloat16)
    pre_act = jnp.dot(normed, weight_in, preferred_element_type=jnp.float32)
    activated = jax.nn.silu(pre_act).astype(jnp.bfloat16)
    return (widened, inverse_rms, normed, pre_act, activated)


def advance(hidden, weight_in, weight_out):
    widened, inverse_rms, normed, pre_act, activated = prepare(hidden, weight_in)
    return (widened + jnp.dot(activated, weight_out, preferred_element_type=jnp.float32)).astype(
        jnp.bfloat16
    )


def retreat(hidden, cot_in, weight_in, weight_out):
    widened, inverse_rms, normed, pre_act, activated = prepare(hidden, weight_in)
    act_grad = contract_last(cot_in, weight_out)
    sigmoid_vals = jax.nn.sigmoid(pre_act)
    pre_grad = (act_grad * sigmoid_vals * (1.0 + pre_act * (1.0 - sigmoid_vals))).astype(
        jnp.bfloat16
    )
    norm_grad = contract_last(pre_grad, weight_in)
    unit_rows = widened * inverse_rms
    rms_grad = inverse_rms * (
        norm_grad - unit_rows * jnp.mean(norm_grad * unit_rows, axis=-1, keepdims=True)
    )
    earlier = (cot_in.astype(jnp.float32) + rms_grad).astype(jnp.bfloat16)
    return (earlier, contract_first(normed, pre_grad), contract_first(activated, cot_in))


def shards(hidden_in, out_grad, fast_in, fast_out, slow_in, slow_out):
    sections = lax.axis_size("section")
    section_index = lax.axis_index("section")
    row_count, model_width = hidden_in.shape
    branch_units = fast_in.shape[2]
    in_scale = 1.0 / math.sqrt(model_width)
    out_scale = 1.0 / math.sqrt(branch_units)
    local_in = (fast_in[0] * in_scale).astype(jnp.bfloat16)
    local_out = (fast_out[0] * out_scale).astype(jnp.bfloat16)
    weight_in, weight_out = (
        lax.all_gather(local_in, "fsdp", axis=0, tiled=True),
        lax.all_gather(local_out, "fsdp", axis=1, tiled=True),
    )
    portions = 1
    block_rows = row_count // portions
    turn_count = sections + portions - 1
    sources = hidden_in.reshape(portions, block_rows, model_width)
    targets = out_grad.reshape(portions, block_rows, model_width)
    saved_inputs = jnp.zeros_like(sources)
    produced = jnp.zeros_like(sources)
    incoming = jnp.zeros((block_rows, model_width), jnp.bfloat16)
    for timestep in range(turn_count):
        block_slot = timestep - section_index
        active = (block_slot >= 0) & (block_slot < portions)
        block_index = jnp.clip(block_slot, 0, portions - 1)
        first_input = lax.dynamic_index_in_dim(sources, block_index, 0, keepdims=False)
        section_input = jnp.where(section_index == 0, first_input, incoming)

        def run_forward():
            return advance(section_input, weight_in, weight_out)

        def skip_forward():
            return jnp.zeros_like(section_input)

        section_output = lax.cond(active, run_forward, skip_forward)
        saved_inputs = jnp.where(
            active,
            lax.dynamic_update_index_in_dim(saved_inputs, section_input, block_index, 0),
            saved_inputs,
        )
        produced = jnp.where(
            active,
            lax.dynamic_update_index_in_dim(produced, section_output, block_index, 0),
            produced,
        )
        if timestep + 1 < turn_count:
            incoming = from_behind(section_output, "section", 1)
    grad_in = jnp.zeros((model_width, branch_units), jnp.float32)
    grad_out = jnp.zeros((branch_units, model_width), jnp.float32)
    cotangents = jnp.zeros_like(sources)
    incoming = jnp.zeros((block_rows, model_width), jnp.bfloat16)
    for timestep in range(turn_count):
        block_slot = timestep - (sections - 1 - section_index)
        active = (block_slot >= 0) & (block_slot < portions)
        block_index = jnp.clip(block_slot, 0, portions - 1)
        last_cot = lax.dynamic_index_in_dim(targets, block_index, 0, keepdims=False)
        cot_in = jnp.where(section_index == sections - 1, last_cot, incoming)
        hidden = lax.dynamic_index_in_dim(saved_inputs, block_index, 0, keepdims=False)

        def run_backward():
            return retreat(hidden, cot_in, weight_in, weight_out)

        def skip_backward():
            return (
                jnp.zeros_like(cot_in),
                jnp.zeros((model_width, branch_units), jnp.float32),
                jnp.zeros((branch_units, model_width), jnp.float32),
            )

        earlier, term_in, term_out = lax.cond(active, run_backward, skip_backward)
        grad_in = grad_in + term_in
        grad_out = grad_out + term_out
        cotangents = jnp.where(
            active, lax.dynamic_update_index_in_dim(cotangents, earlier, block_index, 0), cotangents
        )
        if timestep + 1 < turn_count:
            incoming = from_behind(earlier, "section", -1)
    shard_in, shard_out = (
        lax.psum_scatter(
            (grad_in * in_scale).astype(jnp.bfloat16), "fsdp", scatter_dimension=0, tiled=True
        ).astype(jnp.float32),
        lax.psum_scatter(
            (grad_out * out_scale).astype(jnp.bfloat16), "fsdp", scatter_dimension=1, tiled=True
        ).astype(jnp.float32),
    )
    fresh_in = fast_in[0] - fast_rate * shard_in
    fresh_out = fast_out[0] - fast_rate * shard_out
    synced_first = slow_in[0] + preview_mix * (fresh_in - slow_in[0])
    synced_second = slow_out[0] + preview_mix * (fresh_out - slow_out[0])
    section_out = produced.reshape(row_count, model_width)[None]
    input_grad = cotangents.reshape(row_count, model_width)[None]
    return (section_out, input_grad, synced_first[None], synced_second[None])


def solution(mesh):
    placed = (
        P("fsdp", None),
        P("fsdp", None),
        P("section", "fsdp", None),
        P("section", None, "fsdp"),
        P("section", "fsdp", None),
        P("section", None, "fsdp"),
    )
    return jax.shard_map(
        shards,
        mesh=mesh,
        in_specs=placed,
        out_specs=(
            P("section", "fsdp", None),
            P("section", "fsdp", None),
            P("section", "fsdp", None),
            P("section", None, "fsdp"),
        ),
        check_vma=False,
    )
```

profile of v0, /device:TPU:0, one launch (start us, length us, event | category | flops | bytes accessed | tf_op | source)
XLA Modules:
  0.0 812.1 jit_solution(2471304480929756898)
XLA Ops:
  7.2 3.0 fusion.125
  11.7 126.2 %all-gather.3.cloned.1.call-done = bf16[4096,1024]{1,0:T(8,128)(2,1)} async-done(((bf16[512,1024]{1,0:T(8,128)(2,1)}), bf16[4096,1024]{1,0:T(8,128)(2,1)}) %all-gather.3.cloned.1.call-update) | async-done | bytes 8388624 | tf_op jit(solution)/shard_map/all_gather | solution.py:72
  137.9 125.8 %all-gather.5.cloned.1.call-done = bf16[1024,4096]{1,0:T(8,128)(2,1)} async-done(((bf16[1024,512]{1,0:T(8,128)(2,1)}), bf16[1024,4096]{1,0:T(8,128)(2,1)}) %all-gather.5.cloned.1.call-update) | async-done | bytes 8388624 | tf_op jit(solution)/shard_map/all_gather | solution.py:73
  263.7 8.6 %conditional.8 = (bf16[128,4096]{1,0:T(8,128)(2,1)S(1)}) conditional(s32[]{:T(128)} %convert_element_type.165, () %tuple.67, (bf16[128,4096]{1,0:T(8,128)(2,1)S(1)}, bf16[4096,1024]{1,0:T(8,128)(2,1)}, bf16[1024,4096]{1,0:T(8,128)(2,1)}) %tuple.68), branch_computations={%region_0.1_spmd, %region_1.3_spmd} | conditional | flops 2152857600 | bytes 19925000 | solution.py:96
  264.0 8.3 %fusion = bf16[128,4096]{1,0:T(8,128)(2,1)S(1)} fusion(bf16[1024,4096]{1,0:T(8,128)(2,1)} %get-tuple-element.94, bf16[128,4096]{1,0:T(8,128)(2,1)S(1)} %get-tuple-element.92, bf16[4096,1024]{1,0:T(8,128)(2,1)} %get-tuple-element.93, f32[128]{0:T(128)S(1)} %add_rsqrt_fusion), kind=kOutput, calls=%fused_computation.1 | convolution fusion | flops 2151284736 | bytes 18874880 | tf_op jit(solution)/shard_map/cond/branch_1_fun/dot_general | solution.py:41
  277.1 15.4 %collective-permute-start.1 = (bf16[128,4096]{1,0:T(8,128)(2,1)S(1)}, bf16[128,4096]{1,0:T(8,128)(2,1)S(1)}, u32[]{:S(2)}, u32[]{:S(2)}) collective-permute-start(bf16[128,4096]{1,0:T(8,128)(2,1)S(1)} %get-tuple-element.193), channel_id=1, source_target_pairs={{0,8},{8,16},{16,24},{1,9},{9,17},{17,25},{2,10},{10,18},{18,26},{... | collective-permute-start | bytes 3145736 | tf_op jit(solution)/shard_map/ppermute | solution.py:15
  295.9 12.4 %collective-permute-start.2 = (bf16[128,4096]{1,0:T(8,128)(2,1)S(1)}, bf16[128,4096]{1,0:T(8,128)(2,1)}, u32[]{:S(2)}, u32[]{:S(2)}) collective-permute-start(bf16[128,4096]{1,0:T(8,128)(2,1)S(1)} %get-tuple-element.194), channel_id=1, source_target_pairs={{0,8},{8,16},{16,24},{1,9},{9,17},{17,25},{2,10},{10,18},{18,26},{... | collective-permute-start | bytes 3145736 | tf_op jit(solution)/shard_map/ppermute | solution.py:15
  311.0 16.0 %conditional.12 = (bf16[128,4096]{1,0:T(8,128)(2,1)S(1)}, f32[4096,1024]{1,0:T(8,128)}, f32[1024,4096]{1,0:T(8,128)}) conditional(s32[]{:T(128)} %convert_element_type.171, () %tuple.75, (pred[]{:T(512)}, bf16[128,4096]{1,0:T(8,128)(2,1)S(1)}, bf16[128,4096]{1,0:T(8,128)(2,1)S(1)}, bf16[128,4096]{1,0:T(8,128)(2,1)S(1)}, ...), branch_computations={%region_12.13_spmd, %region_13.16_spmd} | conditional | flops 5382078464 | bytes 136582752 | solution.py:131
  311.1 7.8 broadcast.229
  318.9 7.9 broadcast.228
  328.3 26.4 %collective-permute-done.3 = bf16[128,4096]{1,0:T(8,128)(2,1)} collective-permute-done((bf16[128,4096]{1,0:T(8,128)(2,1)S(1)}, bf16[128,4096]{1,0:T(8,128)(2,1)}, u32[]{:S(2)}, u32[]{:S(2)}) %collective-permute-start.3) | collective-permute-done | bytes 1048608 | tf_op jit(solution)/shard_map/ppermute | solution.py:15
  354.7 17.1 %conditional.13 = (bf16[128,4096]{1,0:T(8,128)(2,1)}, f32[4096,1024]{1,0:T(8,128)}, f32[1024,4096]{1,0:T(8,128)}) conditional(s32[]{:T(128)} %convert_element_type.170, () %tuple.74, (pred[]{:T(512)}, bf16[128,4096]{1,0:T(8,128)(2,1)S(1)}, bf16[128,4096]{1,0:T(8,128)(2,1)}, bf16[128,4096]{1,0:T(8,128)(2,1)S(1)}, bf16[1024,4096]{1,0:T(8,128)(2,1)}, ...), branch_computations={%region_16.17_spmd, %region_17.20_spmd} | conditional | flops 5382078464 | bytes 136582752 | solution.py:131
  355.8 7.8 broadcast.235
  363.6 7.9 broadcast.234
  373.2 15.8 %collective-permute-done.4 = bf16[128,4096]{1,0:T(8,128)(2,1)S(1)} collective-permute-done((bf16[128,4096]{1,0:T(8,128)(2,1)}, bf16[128,4096]{1,0:T(8,128)(2,1)S(1)}, u32[]{:S(2)}, u32[]{:S(2)}) %collective-permute-start.4) | collective-permute-done | bytes 1048608 | tf_op jit(solution)/shard_map/ppermute | solution.py:15
  389.0 16.1 %conditional.14 = (bf16[128,4096]{1,0:T(8,128)(2,1)S(1)}, f32[4096,1024]{1,0:T(8,128)}, f32[1024,4096]{1,0:T(8,128)}) conditional(s32[]{:T(128)} %convert_element_type.169, () %tuple.73, (pred[]{:T(512)}, bf16[128,4096]{1,0:T(8,128)(2,1)S(1)}, bf16[128,4096]{1,0:T(8,128)(2,1)S(1)}, bf16[128,4096]{1,0:T(8,128)(2,1)S(1)}, ...), branch_computations={%region_20.21_spmd, %region_21.24_spmd} | conditional | flops 5382078464 | bytes 136582752 | solution.py:131
  389.3 7.9 broadcast.241
  397.2 7.9 broadcast.240
  406.5 41.1 %collective-permute-done.5 = bf16[128,4096]{1,0:T(8,128)(2,1)} collective-permute-done((bf16[128,4096]{1,0:T(8,128)(2,1)S(1)}, bf16[128,4096]{1,0:T(8,128)(2,1)}, u32[]{:S(2)}, u32[]{:S(2)}) %collective-permute-start.5) | collective-permute-done | bytes 1048608 | tf_op jit(solution)/shard_map/ppermute | solution.py:15
  447.6 31.9 %conditional.15 = (bf16[128,4096]{1,0:T(8,128)(2,1)}, f32[4096,1024]{1,0:T(8,128)}, f32[1024,4096]{1,0:T(8,128)}) conditional(s32[]{:T(128)} %convert_element_type.168, () %tuple.72, (pred[]{:T(512)}, bf16[128,4096]{1,0:T(8,128)(2,1)S(1)}, bf16[128,4096]{1,0:T(8,128)(2,1)}, bf16[128,4096]{1,0:T(8,128)(2,1)S(1)}, bf16[1024,4096]{1,0:T(8,128)(2,1)}, ...), branch_computations={%region_24.25_spmd, %region_25.28_spmd} | conditional | flops 5382078464 | bytes 136582752 | solution.py:131
  449.4 4.8 fusion.115
  455.4 2.9 fusion.112
  458.3 3.0 fusion.105
  462.9 8.1 fusion.117
  471.0 8.2 %fusion.113 = f32[4096,1024]{1,0:T(8,128)} fusion(bf16[128,1024]{1,0:T(8,128)(2,1)S(1)} %fusion.112, bf16[128,4096]{1,0:T(8,128)(2,1)S(1)} %get-tuple-element.125, f32[128]{0:T(128)S(1)} %add_rsqrt_fusion.7), kind=kOutput, calls=%fused_computation.137 | convolution fusion | flops 1075314688 | bytes 18088448 | tf_op jit(solution)/shard_map/cond/branch_1_fun/dot_general | solution.py:25
  479.4 25.8 %multiply_convert_fusion.12 = bf16[1024,4096]{1,0:T(8,128)(2,1)} fusion(f32[1024,4096]{1,0:T(8,128)} %get-tuple-element.155, f32[1024,4096]{1,0:T(8,128)} %get-tuple-element.154, f32[1024,4096]{1,0:T(8,128)} %get-tuple-element.152, f32[1024,4096]{1,0:T(8,128)} %get-tuple-element.153), kind=kLoop, calls=%fused_computation.144 | loop fusion | flops 20971520 | bytes 75497472 | tf_op jit(solution)/shard_map/convert_element_type | solution.py:144
  505.3 26.9 %multiply_convert_fusion.13 = bf16[4096,1024]{1,0:T(8,128)(2,1)} fusion(f32[4096,1024]{1,0:T(8,128)} %get-tuple-element.151, f32[4096,1024]{1,0:T(8,128)} %get-tuple-element.150, f32[4096,1024]{1,0:T(8,128)} %get-tuple-element.148, f32[4096,1024]{1,0:T(8,128)} %get-tuple-element.149), kind=kLoop, calls=%fused_computation.145 | loop fusion | flops 20971520 | bytes 75497472 | tf_op jit(solution)/shard_map/convert_element_type | solution.py:141
  535.0 3.4 select_bitcast_fusion
  538.4 112.1 %reduce-scatter.5.cloned.1.call-done = bf16[1024,512]{1,0:T(8,128)(2,1)} async-done(((bf16[1024,4096]{1,0:T(8,128)(2,1)}), bf16[1024,512]{1,0:T(8,128)(2,1)}) %reduce-scatter.5.cloned.1.call-update) | async-done | bytes 1048592 | tf_op jit(solution)/shard_map/reduce_scatter | solution.py:143
  650.5 3.8 fusion.121
  654.2 146.3 %reduce-scatter.3.cloned.1.call-done = bf16[512,1024]{1,0:T(8,128)(2,1)} async-done(((bf16[4096,1024]{1,0:T(8,128)(2,1)}), bf16[512,1024]{1,0:T(8,128)(2,1)}) %reduce-scatter.3.cloned.1.call-update) | async-done | bytes 1048592 | tf_op jit(solution)/shard_map/reduce_scatter | solution.py:140
  800.6 4.6 fusion.123
  (68 shorter events, 25.2 us)
Async XLA Ops:
  7.2 3.1 copy-start.2
  7.2 130.7 %all-gather.3.cloned.1.call-start = ((), (), s32[]{:S(2)}) async-start(), calls=%async_computation.2 | async-start | bytes 9437184 | tf_op jit(solution)/shard_map/all_gather | solution.py:72
  10.2 1.4 copy-start.1
  10.2 253.5 %all-gather.5.cloned.1.call-start = ((), (), s32[]{:S(2)}) async-start(), calls=%async_computation.3 | async-start | bytes 9437184 | tf_op jit(solution)/shard_map/all_gather | solution.py:73
  11.5 638.9 %reduce-scatter.5.cloned.1.call-start = ((), (), s32[]{:S(2)}) async-start(), calls=%async_computation.5 | async-start | bytes 9437184 | tf_op jit(solution)/shard_map/reduce_scatter | solution.py:143
  272.3 4.7 copy-start.7
  272.3 3.6 collective-permute-start
  277.0 18.7 %copy-start.8 = (bf16[128,4096]{1,0:T(8,128)(2,1)}, bf16[128,4096]{1,0:T(8,128)(2,1)S(1)}, u32[]{:S(2)}) copy-start(bf16[128,4096]{1,0:T(8,128)(2,1)S(1)} %get-tuple-element.193) | copy-start | bytes 3145732
  277.1 17.6 %collective-permute-start.1 = (bf16[128,4096]{1,0:T(8,128)(2,1)S(1)}, bf16[128,4096]{1,0:T(8,128)(2,1)S(1)}, u32[]{:S(2)}, u32[]{:S(2)}) collective-permute-start(bf16[128,4096]{1,0:T(8,128)(2,1)S(1)} %get-tuple-element.193), channel_id=1, source_target_pairs={{0,8},{8,16},{16,24},{1,9},{9,17},{17,25},{2,10},{10,18},{18,26},{... | collective-permute-start | bytes 3145736 | tf_op jit(solution)/shard_map/ppermute | solution.py:15
  295.9 12.4 %copy-start.9 = (bf16[128,4096]{1,0:T(8,128)(2,1)}, bf16[128,4096]{1,0:T(8,128)(2,1)S(1)}, u32[]{:S(2)}) copy-start(bf16[128,4096]{1,0:T(8,128)(2,1)S(1)} %get-tuple-element.194) | copy-start | bytes 3145732
  295.9 13.8 %collective-permute-start.2 = (bf16[128,4096]{1,0:T(8,128)(2,1)S(1)}, bf16[128,4096]{1,0:T(8,128)(2,1)}, u32[]{:S(2)}, u32[]{:S(2)}) collective-permute-start(bf16[128,4096]{1,0:T(8,128)(2,1)S(1)} %get-tuple-element.194), channel_id=1, source_target_pairs={{0,8},{8,16},{16,24},{1,9},{9,17},{17,25},{2,10},{10,18},{18,26},{... | collective-permute-start | bytes 3145736 | tf_op jit(solution)/shard_map/ppermute | solution.py:15
  308.3 2.7 copy-start
  327.0 27.8 %copy-start.4 = (bf16[128,4096]{1,0:T(8,128)(2,1)}, bf16[128,4096]{1,0:T(8,128)(2,1)S(1)}, u32[]{:S(2)}) copy-start(bf16[128,4096]{1,0:T(8,128)(2,1)S(1)} %get-tuple-element.144) | copy-start | bytes 3145732
  327.0 27.8 %collective-permute-start.3 = (bf16[128,4096]{1,0:T(8,128)(2,1)S(1)}, bf16[128,4096]{1,0:T(8,128)(2,1)}, u32[]{:S(2)}, u32[]{:S(2)}) collective-permute-start(bf16[128,4096]{1,0:T(8,128)(2,1)S(1)} %get-tuple-element.144), channel_id=1, source_target_pairs={{8,0},{16,8},{24,16},{9,1},{17,9},{25,17},{10,2},{18,10},{26,18},{... | collective-permute-start | bytes 3145736 | tf_op jit(solution)/shard_map/ppermute | solution.py:15
  371.9 17.2 %collective-permute-start.4 = (bf16[128,4096]{1,0:T(8,128)(2,1)}, bf16[128,4096]{1,0:T(8,128)(2,1)S(1)}, u32[]{:S(2)}, u32[]{:S(2)}) collective-permute-start(bf16[128,4096]{1,0:T(8,128)(2,1)} %get-tuple-element.145), channel_id=1, source_target_pairs={{8,0},{16,8},{24,16},{9,1},{17,9},{25,17},{10,2},{18,10},{26,18},{... | collective-permute-start | bytes 3145736 | tf_op jit(solution)/shard_map/ppermute | solution.py:15
  405.2 42.4 %copy-start.6 = (bf16[128,4096]{1,0:T(8,128)(2,1)}, bf16[128,4096]{1,0:T(8,128)(2,1)S(1)}, u32[]{:S(2)}) copy-start(bf16[128,4096]{1,0:T(8,128)(2,1)S(1)} %get-tuple-element.146) | copy-start | bytes 3145732
  405.2 42.4 %collective-permute-start.5 = (bf16[128,4096]{1,0:T(8,128)(2,1)S(1)}, bf16[128,4096]{1,0:T(8,128)(2,1)}, u32[]{:S(2)}, u32[]{:S(2)}) collective-permute-start(bf16[128,4096]{1,0:T(8,128)(2,1)S(1)} %get-tuple-element.146), channel_id=1, source_target_pairs={{8,0},{16,8},{24,16},{9,1},{17,9},{25,17},{10,2},{18,10},{26,18},{... | collective-permute-start | bytes 3145736 | tf_op jit(solution)/shard_map/ppermute | solution.py:15
  449.1 9.2 %slice-start.6 = ((s8[8388608]{0:T(1024)(128)(4,1)}), s8[4194304]{0:T(1024)(128)(4,1)S(1)}, s32[]{:S(2)}) async-start(s8[8388608]{0:T(1024)(128)(4,1)} %bitcast.82), calls=%async_computation.12 | async-start | bytes 8388608 | tf_op jit(solution)/shard_map/cond
  449.4 5.9 copy-start.15
  449.4 8.9 %slice-start.7 = ((s8[8388608]{0:T(1024)(128)(4,1)}), s8[4194304]{0:T(1024)(128)(4,1)S(1)}, s32[]{:S(2)}) async-start(s8[8388608]{0:T(1024)(128)(4,1)} %bitcast.82), calls=%async_computation.13 | async-start | bytes 8388608 | tf_op jit(solution)/shard_map/cond
  505.2 295.3 %reduce-scatter.3.cloned.1.call-start = ((), (), s32[]{:S(2)}) async-start(), calls=%async_computation.4 | async-start | bytes 9437184 | tf_op jit(solution)/shard_map/reduce_scatter | solution.py:140
  532.1 1.2 copy-start.11
  533.4 1.6 copy-start.5
  533.5 1.0 copy-start.10
  535.0 115.5 %copy-start.3 = (f32[1,1024,512]{2,1,0:T(8,128)S(1)}, f32[1,1024,512]{2,1,0:T(8,128)}, u32[]{:S(2)}) copy-start(f32[1,1024,512]{2,1,0:T(8,128)} %param.25) | copy-start | bytes 6291460
Sparse Core Ops, SparseCore 0:
  10.7 127.1 all-gather.2
  140.5 123.1 all-gather.4
  505.4 145.0 reduce-scatter.4
  654.0 146.5 reduce-scatter.2
where the time goes:
time: 821 us; the launch traced here: 812 us
  waiting for transfers between devices  600 us (73%)
  other arithmetic  75.5 us (9%)
  local copies, waits for them, and re-layouts  52.8 us (6%)
  matrix products  35.3 us (4%)
  starting transfers between devices  33.2 us (4%)
  between operations  14.5 us (2%)
    reduce_scatter x1, waiting for transfers between devices, shards(): lax.psum_scatter((grad_in * in_scale).astype(jnp.bfloat16), 'fsdp', scatt...  146 us
    all_gather x1, waiting for transfers between devices, shards(): lax.all_gather(local_in, 'fsdp', axis=0, tiled=True)  126 us
    all_gather x1, waiting for transfers between devices, shards(): lax.all_gather(local_out, 'fsdp', axis=1, tiled=True)  126 us
    reduce_scatter x1, waiting for transfers between devices, shards(): lax.psum_scatter((grad_out * out_scale).astype(jnp.bfloat16), 'fsdp', sca...  112 us
    ppermute x6, waiting for transfers between devices, from_behind(): lax.ppermute(value, axis, [(source, source + steps) for source in range(l...  89.1 us
    another operation x13, local copies, waits for them, and re-layouts  48.9 us
    ppermute x6, starting transfers between devices, from_behind(): lax.ppermute(value, axis, [(source, source + steps) for source in range(l...  33 us
    convert_element_type x1, other arithmetic, shards(): (grad_in * in_scale).astype(jnp.bfloat16)  26.9 us
  transfers between devices with their start and end apart: 10, of which 10 were waited for; matrix products, arithmetic and copies ran while one was open for 4% of the time, Pallas kernels for 0%

commit v1 on v0

--- a/solution.py
+++ b/solution.py
@@ -7,6 +7,28 @@
 epsilon = 1e-05
 fast_rate = 0.5
 preview_mix = 0.5
+
+
+def joined_along(blocks, dim):
+    blocks = jnp.moveaxis(blocks, 0, dim)
+    shape = blocks.shape
+    return blocks.reshape(*shape[:dim], shape[dim] * shape[dim + 1], *shape[dim + 2 :])
+
+
+def doubled(shard, axis):
+    peers = lax.axis_size(axis)
+    tiles = shard[None]
+    for level in range(peers.bit_length() - 1):
+        stride = 1 << level
+        other = lax.ppermute(tiles, axis, [(i, i ^ stride) for i in range(peers)])
+        both = jnp.stack([tiles, other])
+        upper = lax.axis_index(axis) >> level & 1
+        tiles = jnp.where(upper == 0, both, both[::-1]).reshape(-1, *shard.shape)
+    return tiles
+
+
+def doubled_up(x, axis, dim):
+    return joined_along(doubled(x, axis), dim)
 
 
 def from_behind(value, axis, steps):
@@ -69,7 +91,7 @@
     local_in = (fast_in[0] * in_scale).astype(jnp.bfloat16)
     local_out = (fast_out[0] * out_scale).astype(jnp.bfloat16)
     weight_in, weight_out = (
-        lax.all_gather(local_in, "fsdp", axis=0, tiled=True),
+        doubled_up(local_in, "fsdp", 0),
         lax.all_gather(local_out, "fsdp", axis=1, tiled=True),
     )
     portions = 1

time: 821 us -> 943 us (1.15)
  waiting for transfers between devices: 600 us -> 689 us
  other arithmetic: 75.5 us -> 104 us
    ppermute x0 -> x3, waiting for transfers between devices: none -> 341 us  [doubled(): other = lax.ppermute(tiles, axis, [(i, i ^ stride) for i in range(peers)])]
    all_gather x1 -> x0, waiting for transfers between devices: 126 us -> none  [shards(): lax.all_gather(local_in, 'fsdp', axis=0, tiled=True)]
    all_gather x1, waiting for transfers between devices: 126 us -> 0.01 us  [shards(): lax.all_gather(local_out, 'fsdp', axis=1, tiled=True)]
    select_n x0 -> x2, other arithmetic: none -> 16.9 us  [doubled(): tiles = jnp.where(upper == 0, both, both[::-1]).reshape(-1, *shard.shape)]
    another operation x0 -> x4, other arithmetic: none -> 13.1 us  [doubled(): both = jnp.stack([tiles, other])]
  transfers between devices with their start and end apart: 10 -> 12, of which waited for: 10 -> 11; matrix products, arithmetic and copies ran while one was open for 4% -> 7% of each run, Pallas kernels for 0% -> 0%
where the time goes in v1:
time: 943 us; the launch traced here: 934 us
  waiting for transfers between devices  689 us (73%)
  other arithmetic  104 us (11%)
  local copies, waits for them, and re-layouts  51.9 us (6%)
  starting transfers between devices  38.3 us (4%)
  matrix products  35.3 us (4%)
  between operations  14.5 us (2%)
    ppermute x3, waiting for transfers between devices, doubled(): other = lax.ppermute(tiles, axis, [(i, i ^ stride) for i in range(peers)])  341 us
    reduce_scatter x1, waiting for transfers between devices, shards(): lax.psum_scatter((grad_in * in_scale).astype(jnp.bfloat16), 'fsdp', scatt...  146 us
    reduce_scatter x1, waiting for transfers between devices, shards(): lax.psum_scatter((grad_out * out_scale).astype(jnp.bfloat16), 'fsdp', sca...  112 us
    ppermute x6, waiting for transfers between devices, from_behind(): lax.ppermute(value, axis, [(source, source + steps) for source in range(l...  89.1 us
    another operation x13, local copies, waits for them, and re-layouts  49.9 us
    ppermute x6, starting transfers between devices, from_behind(): lax.ppermute(value, axis, [(source, source + steps) for source in range(l...  33.2 us
    convert_element_type x1, other arithmetic, shards(): (grad_in * in_scale).astype(jnp.bfloat16)  27 us
    convert_element_type x1, other arithmetic, shards(): (grad_out * out_scale).astype(jnp.bfloat16)  25.8 us
  transfers between devices with their start and end apart: 12, of which 11 were waited for; matrix products, arithmetic and copies ran while one was open for 7% of the time, Pallas kernels for 0%

profile of v1, /device:TPU:0, one launch (start us, length us, event | category | flops | bytes accessed | tf_op | source)
XLA Modules:
  0.0 934.4 jit_solution(16133485487923479517)
XLA Ops:
  13.8 34.2 %collective-permute-done = bf16[1,512,1024]{2,1,0:T(8,128)(2,1)} collective-permute-done((bf16[1,512,1024]{2,1,0:T(8,128)(2,1)S(1)}, bf16[1,512,1024]{2,1,0:T(8,128)(2,1)}, u32[]{:S(2)}, u32[]{:S(2)}) %collective-permute-start) | collective-permute-done | bytes 1048608 | tf_op jit(solution)/shard_map/ppermute | solution.py:23
  53.5 95.5 %collective-permute-done.1 = bf16[2,512,1024]{2,1,0:T(8,128)(2,1)} collective-permute-done((bf16[2,512,1024]{2,1,0:T(8,128)(2,1)}, bf16[2,512,1024]{2,1,0:T(8,128)(2,1)}, u32[]{:S(2)}, u32[]{:S(2)}) %collective-permute-start.1) | collective-permute-done | bytes 2097184 | tf_op jit(solution)/shard_map/ppermute | solution.py:23
  151.0 3.2 reverse_select_fusion.1
  154.5 211.7 %collective-permute-done.2 = bf16[4,512,1024]{2,1,0:T(8,128)(2,1)} collective-permute-done((bf16[4,512,1024]{2,1,0:T(8,128)(2,1)}, bf16[4,512,1024]{2,1,0:T(8,128)(2,1)}, u32[]{:S(2)}, u32[]{:S(2)}) %collective-permute-start.2) | collective-permute-done | bytes 4194336 | tf_op jit(solution)/shard_map/ppermute | solution.py:23
  366.2 7.5 pad_maximum_fusion
  373.7 13.7 %reverse_select_fusion = bf16[2,4,512,1024]{3,2,1,0:T(8,128)(2,1)} fusion(bf16[2,4,512,1024]{3,2,1,0:T(8,128)(2,1)} %pad_maximum_fusion, pred[]{:T(512)S(6)} %eq.22), kind=kLoop, calls=%fused_computation.146 | loop fusion | flops 4194304 | bytes 16777216 | tf_op jit(solution)/shard_map/jit(_where)/select_n | solution.py:26
  387.3 8.6 conditional.8
  387.6 8.3 fusion
  400.9 15.4 %collective-permute-start.4 = (bf16[128,4096]{1,0:T(8,128)(2,1)S(1)}, bf16[128,4096]{1,0:T(8,128)(2,1)S(1)}, u32[]{:S(2)}, u32[]{:S(2)}) collective-permute-start(bf16[128,4096]{1,0:T(8,128)(2,1)S(1)} %get-tuple-element.195), channel_id=1, source_target_pairs={{0,8},{8,16},{16,24},{1,9},{9,17},{17,25},{2,10},{10,18},{18,26},{... | collective-permute-start | bytes 3145736 | tf_op jit(solution)/shard_map/ppermute | solution.py:37
  419.7 12.4 %collective-permute-start.5 = (bf16[128,4096]{1,0:T(8,128)(2,1)S(1)}, bf16[128,4096]{1,0:T(8,128)(2,1)}, u32[]{:S(2)}, u32[]{:S(2)}) collective-permute-start(bf16[128,4096]{1,0:T(8,128)(2,1)S(1)} %get-tuple-element.196), channel_id=1, source_target_pairs={{0,8},{8,16},{16,24},{1,9},{9,17},{17,25},{2,10},{10,18},{18,26},{... | collective-permute-start | bytes 3145736 | tf_op jit(solution)/shard_map/ppermute | solution.py:37
  434.8 16.0 %conditional.12 = (bf16[128,4096]{1,0:T(8,128)(2,1)S(1)}, f32[4096,1024]{1,0:T(8,128)}, f32[1024,4096]{1,0:T(8,128)}) conditional(s32[]{:T(128)} %convert_element_type.183, () %tuple.75, (pred[]{:T(512)}, bf16[128,4096]{1,0:T(8,128)(2,1)S(1)}, bf16[128,4096]{1,0:T(8,128)(2,1)S(1)}, bf16[128,4096]{1,0:T(8,128)(2,1)S(1)}, ...), branch_computations={%region_12.13_spmd, %region_13.16_spmd} | conditional | flops 5382078464 | bytes 136582752 | solution.py:153
  434.9 7.8 broadcast.239
  442.7 7.9 broadcast.238
  452.1 26.4 %collective-permute-done.6 = bf16[128,4096]{1,0:T(8,128)(2,1)} collective-permute-done((bf16[128,4096]{1,0:T(8,128)(2,1)S(1)}, bf16[128,4096]{1,0:T(8,128)(2,1)}, u32[]{:S(2)}, u32[]{:S(2)}) %collective-permute-start.6) | collective-permute-done | bytes 1048608 | tf_op jit(solution)/shard_map/ppermute | solution.py:37
  478.6 17.2 %conditional.13 = (bf16[128,4096]{1,0:T(8,128)(2,1)}, f32[4096,1024]{1,0:T(8,128)}, f32[1024,4096]{1,0:T(8,128)}) conditional(s32[]{:T(128)} %convert_element_type.182, () %tuple.74, (pred[]{:T(512)}, bf16[128,4096]{1,0:T(8,128)(2,1)S(1)}, bf16[128,4096]{1,0:T(8,128)(2,1)}, bf16[128,4096]{1,0:T(8,128)(2,1)S(1)}, bf16[1024,4096]{1,0:T(8,128)(2,1)}, ...), branch_computations={%region_16.17_spmd, %region_17.20_spmd} | conditional | flops 5382078464 | bytes 136582752 | solution.py:153
  479.7 7.8 broadcast.245
  487.5 7.9 broadcast.244
  497.1 15.8 %collective-permute-done.7 = bf16[128,4096]{1,0:T(8,128)(2,1)S(1)} collective-permute-done((bf16[128,4096]{1,0:T(8,128)(2,1)}, bf16[128,4096]{1,0:T(8,128)(2,1)S(1)}, u32[]{:S(2)}, u32[]{:S(2)}) %collective-permute-start.7) | collective-permute-done | bytes 1048608 | tf_op jit(solution)/shard_map/ppermute | solution.py:37
  513.0 16.1 %conditional.14 = (bf16[128,4096]{1,0:T(8,128)(2,1)S(1)}, f32[4096,1024]{1,0:T(8,128)}, f32[1024,4096]{1,0:T(8,128)}) conditional(s32[]{:T(128)} %convert_element_type.181, () %tuple.73, (pred[]{:T(512)}, bf16[128,4096]{1,0:T(8,128)(2,1)S(1)}, bf16[128,4096]{1,0:T(8,128)(2,1)S(1)}, bf16[128,4096]{1,0:T(8,128)(2,1)S(1)}, ...), branch_computations={%region_20.21_spmd, %region_21.24_spmd} | conditional | flops 5382078464 | bytes 136582752 | solution.py:153
  513.2 7.9 broadcast.251
  521.1 8.0 broadcast.250
  530.4 41.1 %collective-permute-done.8 = bf16[128,4096]{1,0:T(8,128)(2,1)} collective-permute-done((bf16[128,4096]{1,0:T(8,128)(2,1)S(1)}, bf16[128,4096]{1,0:T(8,128)(2,1)}, u32[]{:S(2)}, u32[]{:S(2)}) %collective-permute-start.8) | collective-permute-done | bytes 1048608 | tf_op jit(solution)/shard_map/ppermute | solution.py:37
  571.4 31.9 %conditional.15 = (bf16[128,4096]{1,0:T(8,128)(2,1)}, f32[4096,1024]{1,0:T(8,128)}, f32[1024,4096]{1,0:T(8,128)}) conditional(s32[]{:T(128)} %convert_element_type.180, () %tuple.72, (pred[]{:T(512)}, bf16[128,4096]{1,0:T(8,128)(2,1)S(1)}, bf16[128,4096]{1,0:T(8,128)(2,1)}, bf16[128,4096]{1,0:T(8,128)(2,1)S(1)}, bf16[1024,4096]{1,0:T(8,128)(2,1)}, ...), branch_computations={%region_24.25_spmd, %region_25.28_spmd} | conditional | flops 5382078464 | bytes 136582752 | solution.py:153
  573.3 4.8 fusion.115
  586.8 8.1 fusion.117
  594.9 8.2 fusion.113
  603.3 25.8 %multiply_convert_fusion.12 = bf16[1024,4096]{1,0:T(8,128)(2,1)} fusion(f32[1024,4096]{1,0:T(8,128)} %get-tuple-element.155, f32[1024,4096]{1,0:T(8,128)} %get-tuple-element.154, f32[1024,4096]{1,0:T(8,128)} %get-tuple-element.152, f32[1024,4096]{1,0:T(8,128)} %get-tuple-element.153), kind=kLoop, calls=%fused_computation.144 | loop fusion | flops 20971520 | bytes 75497472 | tf_op jit(solution)/shard_map/convert_element_type | solution.py:166
  629.2 27.0 %multiply_convert_fusion.13 = bf16[4096,1024]{1,0:T(8,128)(2,1)} fusion(f32[4096,1024]{1,0:T(8,128)} %get-tuple-element.151, f32[4096,1024]{1,0:T(8,128)} %get-tuple-element.150, f32[4096,1024]{1,0:T(8,128)} %get-tuple-element.148, f32[4096,1024]{1,0:T(8,128)} %get-tuple-element.149), kind=kLoop, calls=%fused_computation.145 | loop fusion | flops 20971520 | bytes 75497472 | tf_op jit(solution)/shard_map/convert_element_type | solution.py:163
  661.1 112.3 %reduce-scatter.5.cloned.1.call-done = bf16[1024,512]{1,0:T(8,128)(2,1)} async-done(((bf16[1024,4096]{1,0:T(8,128)(2,1)}), bf16[1024,512]{1,0:T(8,128)(2,1)}) %reduce-scatter.5.cloned.1.call-update) | async-done | bytes 1048592 | tf_op jit(solution)/shard_map/reduce_scatter | solution.py:165
  773.4 4.4 fusion.121
  777.8 145.8 %reduce-scatter.3.cloned.1.call-done = bf16[512,1024]{1,0:T(8,128)(2,1)} async-done(((bf16[4096,1024]{1,0:T(8,128)(2,1)}), bf16[512,1024]{1,0:T(8,128)(2,1)}) %reduce-scatter.3.cloned.1.call-update) | async-done | bytes 1048592 | tf_op jit(solution)/shard_map/reduce_scatter | solution.py:162
  923.7 3.7 fusion.125
  (74 shorter events, 47.1 us)
Async XLA Ops:
  7.2 3.1 copy-start
  7.2 380.2 %all-gather.2.cloned.1.call-start = ((), (), s32[]{:S(2)}) async-start(), calls=%async_computation.2 | async-start | bytes 9437184 | tf_op jit(solution)/shard_map/all_gather | solution.py:95
  10.2 763.2 %reduce-scatter.5.cloned.1.call-start = ((), (), s32[]{:S(2)}) async-start(), calls=%async_computation.4 | async-start | bytes 9437184 | tf_op jit(solution)/shard_map/reduce_scatter | solution.py:165
  10.5 37.5 %collective-permute-start = (bf16[1,512,1024]{2,1,0:T(8,128)(2,1)S(1)}, bf16[1,512,1024]{2,1,0:T(8,128)(2,1)}, u32[]{:S(2)}, u32[]{:S(2)}) collective-permute-start(bf16[1,512,1024]{2,1,0:T(8,128)(2,1)S(1)} %multiply_convert_fusion.14), channel_id=1, source_target_pairs={{0,1},{1,0},{2,3},{3,2},{4,5},{5,4},{6,7},{7,6},{8,9},{9,8},{10,11... | collective-permute-start | bytes 3145736 | tf_op jit(solution)/shard_map/ppermute | solution.py:23
  51.7 97.4 %collective-permute-start.1 = (bf16[2,512,1024]{2,1,0:T(8,128)(2,1)}, bf16[2,512,1024]{2,1,0:T(8,128)(2,1)}, u32[]{:S(2)}, u32[]{:S(2)}) collective-permute-start(bf16[2,512,1024]{2,1,0:T(8,128)(2,1)} %get-tuple-element.167), channel_id=1, source_target_pairs={{0,2},{1,3},{2,0},{3,1},{4,6},{5,7},{6,4},{7,5},{8,10},{9,11},{10,... | collective-permute-start | bytes 6291464 | tf_op jit(solution)/shard_map/ppermute | solution.py:23
  151.0 3.4 copy-start.3
  154.2 211.9 %collective-permute-start.2 = (bf16[4,512,1024]{2,1,0:T(8,128)(2,1)}, bf16[4,512,1024]{2,1,0:T(8,128)(2,1)}, u32[]{:S(2)}, u32[]{:S(2)}) collective-permute-start(bf16[4,512,1024]{2,1,0:T(8,128)(2,1)} %bitcast.6), channel_id=1, source_target_pairs={{0,4},{1,5},{2,6},{3,7},{4,0},{5,1},{6,2},{7,3},{8,12},{9,13},{10,... | collective-permute-start | bytes 12582920 | tf_op jit(solution)/shard_map/ppermute | solution.py:23
  395.9 4.8 copy-start.6
  395.9 3.7 collective-permute-start.3
  400.9 18.7 %copy-start.8 = (bf16[128,4096]{1,0:T(8,128)(2,1)}, bf16[128,4096]{1,0:T(8,128)(2,1)S(1)}, u32[]{:S(2)}) copy-start(bf16[128,4096]{1,0:T(8,128)(2,1)S(1)} %get-tuple-element.195) | copy-start | bytes 3145732
  400.9 17.6 %collective-permute-start.4 = (bf16[128,4096]{1,0:T(8,128)(2,1)S(1)}, bf16[128,4096]{1,0:T(8,128)(2,1)S(1)}, u32[]{:S(2)}, u32[]{:S(2)}) collective-permute-start(bf16[128,4096]{1,0:T(8,128)(2,1)S(1)} %get-tuple-element.195), channel_id=1, source_target_pairs={{0,8},{8,16},{16,24},{1,9},{9,17},{17,25},{2,10},{10,18},{18,26},{... | collective-permute-start | bytes 3145736 | tf_op jit(solution)/shard_map/ppermute | solution.py:37
  419.7 12.4 %copy-start.9 = (bf16[128,4096]{1,0:T(8,128)(2,1)}, bf16[128,4096]{1,0:T(8,128)(2,1)S(1)}, u32[]{:S(2)}) copy-start(bf16[128,4096]{1,0:T(8,128)(2,1)S(1)} %get-tuple-element.196) | copy-start | bytes 3145732
  419.7 13.8 %collective-permute-start.5 = (bf16[128,4096]{1,0:T(8,128)(2,1)S(1)}, bf16[128,4096]{1,0:T(8,128)(2,1)}, u32[]{:S(2)}, u32[]{:S(2)}) collective-permute-start(bf16[128,4096]{1,0:T(8,128)(2,1)S(1)} %get-tuple-element.196), channel_id=1, source_target_pairs={{0,8},{8,16},{16,24},{1,9},{9,17},{17,25},{2,10},{10,18},{18,26},{... | collective-permute-start | bytes 3145736 | tf_op jit(solution)/shard_map/ppermute | solution.py:37
  432.1 2.7 copy-start.2
  450.8 27.8 %copy-start.4 = (bf16[128,4096]{1,0:T(8,128)(2,1)}, bf16[128,4096]{1,0:T(8,128)(2,1)S(1)}, u32[]{:S(2)}) copy-start(bf16[128,4096]{1,0:T(8,128)(2,1)S(1)} %get-tuple-element.144) | copy-start | bytes 3145732
  450.8 27.8 %collective-permute-start.6 = (bf16[128,4096]{1,0:T(8,128)(2,1)S(1)}, bf16[128,4096]{1,0:T(8,128)(2,1)}, u32[]{:S(2)}, u32[]{:S(2)}) collective-permute-start(bf16[128,4096]{1,0:T(8,128)(2,1)S(1)} %get-tuple-element.144), channel_id=1, source_target_pairs={{8,0},{16,8},{24,16},{9,1},{17,9},{25,17},{10,2},{18,10},{26,18},{... | collective-permute-start | bytes 3145736 | tf_op jit(solution)/shard_map/ppermute | solution.py:37
  495.8 17.2 %collective-permute-start.7 = (bf16[128,4096]{1,0:T(8,128)(2,1)}, bf16[128,4096]{1,0:T(8,128)(2,1)S(1)}, u32[]{:S(2)}, u32[]{:S(2)}) collective-permute-start(bf16[128,4096]{1,0:T(8,128)(2,1)} %get-tuple-element.145), channel_id=1, source_target_pairs={{8,0},{16,8},{24,16},{9,1},{17,9},{25,17},{10,2},{18,10},{26,18},{... | collective-permute-start | bytes 3145736 | tf_op jit(solution)/shard_map/ppermute | solution.py:37
  529.1 42.4 %collective-permute-start.8 = (bf16[128,4096]{1,0:T(8,128)(2,1)S(1)}, bf16[128,4096]{1,0:T(8,128)(2,1)}, u32[]{:S(2)}, u32[]{:S(2)}) collective-permute-start(bf16[128,4096]{1,0:T(8,128)(2,1)S(1)} %get-tuple-element.146), channel_id=1, source_target_pairs={{8,0},{16,8},{24,16},{9,1},{17,9},{25,17},{10,2},{18,10},{26,18},{... | collective-permute-start | bytes 3145736 | tf_op jit(solution)/shard_map/ppermute | solution.py:37
  573.0 9.2 slice-start.6
  573.3 5.9 copy-start.13
  573.3 8.9 slice-start.7
  629.1 294.6 %reduce-scatter.3.cloned.1.call-start = ((), (), s32[]{:S(2)}) async-start(), calls=%async_computation.3 | async-start | bytes 9437184 | tf_op jit(solution)/shard_map/reduce_scatter | solution.py:162
  656.2 1.6 copy-start.5
  656.2 2.0 copy-start.7
  661.1 262.6 %copy-start.1 = (f32[1,512,1024]{2,1,0:T(8,128)S(1)}, f32[1,512,1024]{2,1,0:T(8,128)}, u32[]{:S(2)}) copy-start(f32[1,512,1024]{2,1,0:T(8,128)} %param.24) | copy-start | bytes 6291460
Sparse Core Ops, SparseCore 0:
  10.6 283.7 all-gather.1
  629.2 144.1 reduce-scatter.4
  777.1 146.5 reduce-scatter.2
